TPU v7x, 32 devices: a whole 2x2x4 slice. The times are simulated.
32 devices in a mesh: fac: 8 (over y, x, core), freq: 4 (over z).
Axes of the slice: x: 2, y: 2, z: 4, core: 2. Of those that a mesh axis runs over, the one named last changes fastest.
Arguments:
- right_side: float32 [16, 36864, 128], P('freq', 'fac'), may hold values from -6 to 6
- factors: bfloat16 [36864, 1024], P('fac'), may hold values from -0.03125 to 0.03125
- pair_weight: float32 [16, 36864], P('freq', 'fac'), may hold values from -2 to 2
- second_order: float32 [16, 36864], P('freq', 'fac'), may hold values from -1 to 1
- forward: float32 [16, 16], replicated, may hold values from -3 to 3
- backward: float32 [16, 16], replicated, may hold values from -3 to 3
Outputs:
- amplitude: float32 [16, 36864, 128], P('freq', 'fac')
- sources: float32 [16, 36864, 128], P('freq', 'fac')
All inputs are finite; a program needn't handle non-finite values.
Results may differ from a plain program's by a relative error of at most 0.0015.
Values may be sent and summed in bfloat16 or wider, within the bound.
A program may use at most 128 MiB of HBM per device.

v0:
```python
import jax
import jax.numpy as jnp
from jax import lax
from jax.sharding import PartitionSpec as P

OUTER = 2
INNER = 2


def shards(right_side, factors, pair_weight, second_order, forward, backward):
    weight = pair_weight[:, :, None]
    sources = right_side
    amplitude = sources
    for outer in range(OUTER):
        amplitude = sources
        for inner in range(INNER):
            rounded = amplitude.astype(jnp.bfloat16)
            partial_value = jnp.einsum(
                "pa,fpc->fac", factors, rounded, preferred_element_type=jnp.float32
            )
            projected = lax.psum(partial_value, "fac").astype(jnp.bfloat16)
            spread = jnp.einsum(
                "pa,fac->fpc", factors, projected, preferred_element_type=jnp.float32
            )
            amplitude = sources + weight * spread
        moved, kernel_rows = (
            lax.all_to_all(amplitude, "freq", split_axis=1, concat_axis=0, tiled=True),
            lax.all_to_all(second_order, "freq", split_axis=1, concat_axis=0, tiled=True),
        )
        timed = jnp.einsum("tw,wpc->tpc", forward, moved, precision=lax.Precision.HIGHEST)
        product = kernel_rows[:, :, None] * timed
        renewed = jnp.einsum("wt,tpc->wpc", backward, product, precision=lax.Precision.HIGHEST)
        returned = lax.all_to_all(renewed, "freq", split_axis=0, concat_axis=1, tiled=True)
        sources = right_side + returned
    return (amplitude, sources)


def solution(mesh):
    return jax.shard_map(
        shards,
        mesh=mesh,
        in_specs=(
            P("freq", "fac", None),
            P("fac", None),
            P("freq", "fac"),
            P("freq", "fac"),
            P(),
            P(),
        ),
        out_specs=(P("freq", "fac", None), P("freq", "fac", None)),
        check_vma=False,
    )
```

profile of v0, /device:TPU:3, one launch (start us, length us, event | category | flops | bytes accessed | tf_op | source)
XLA Modules:
  0.0 1309.2 jit_solution(18389353184218481441)
XLA Ops:
  0.6 4.6 all-to-all-start
  5.2 9.6 copy.50
  14.8 10.4 fusion.42
  25.3 57.3 %all-reduce.4 = bf16[4,1024,128]{1,2,0:T(8,128)(2,1)S(1)} all-reduce(f32[4,1024,128]{1,2,0:T(8,128)S(1)} %fusion.42), channel_id=1, replica_groups=mesh['fac'=8,'freq'=4] {'fac'}, use_global_device_ids=true, to_apply=%region_0.0 | all-reduce | flops 524288 | bytes 3145728 | tf_op jit(solution)/shard_map/psum | solution.py:21
  82.5 19.6 %fusion.52 = f32[4,1024,128]{1,2,0:T(8,128)S(1)} fusion(bf16[4608,1024]{1,0:T(8,128)(2,1)} %param.7, f32[4,4608,128]{1,2,0:T(8,128)} %copy.50, f32[4,4608]{1,0:T(4,128)S(1)} %copy-done.4, bf16[4,1024,128]{1,2,0:T(8,128)(2,1)S(1)} %all-reduce.4), kind=kOutput, calls=%fused_computation.39 | convolution fusion | flops 9670754304 | bytes 22093824 | tf_op jit(solution)/shard_map/pa,fpc->fac/dot_general | solution.py:18
  102.1 56.3 %all-reduce.5 = bf16[4,1024,128]{1,2,0:T(8,128)(2,1)S(1)} all-reduce(f32[4,1024,128]{1,2,0:T(8,128)S(1)} %fusion.52), channel_id=1, replica_groups=mesh['fac'=8,'freq'=4] {'fac'}, use_global_device_ids=true, to_apply=%region_1.0 | all-reduce | flops 524288 | bytes 3145728 | tf_op jit(solution)/shard_map/psum | solution.py:21
  158.5 12.6 bitcast_add_fusion.3
  171.1 11.9 copy.44
  183.0 6.0 all-to-all-start.1
  190.1 203.0 %all-to-all-done.1 = f32[4,4608,128]{2,0,1:T(4,128)} async-done(((f32[4,4608,128]{2,0,1:T(4,128)}), f32[4,4608,128]{2,0,1:T(4,128)}, u32[]{:S(2)}, u32[]{:S(2)}) %all-to-all-start.1) | async-done | bytes 9437216 | tf_op jit(solution)/shard_map/all_to_all | solution.py:27
  393.1 4.3 copy.45
  398.3 13.9 %fusion.22 = f32[1152,128,16]{1,2,0:T(8,128)S(1)} fusion(f32[16,1152,128]{2,1,0:T(8,128)S(1)} %bitcast.117, f32[16,16]{1,0:T(8,128)S(1)} %copy-done), kind=kOutput, calls=%fused_computation.29 | convolution fusion | flops 452984832 | bytes 18875392 | tf_op jit(solution)/shard_map/tw,wpc->tpc/dot_general | solution.py:30
  412.2 10.5 fusion.36
  425.8 210.0 %all_to_all.93 = f32[16,1152,128]{2,1,0:T(8,128)} all-to-all(f32[16,1152,128]{2,1,0:T(8,128)S(1)} %copy.48), channel_id=1, replica_groups=mesh['fac'=8,'freq'=4] {'freq'}, dimensions={0} | all-to-all | bytes 18874368 | tf_op jit(solution)/shard_map/all_to_all | solution.py:33
  635.7 11.9 copy.49
  647.6 11.3 all_to_all.79
  658.9 11.8 add.28
  670.7 10.3 fusion.47
  681.0 55.8 %all-reduce.6 = bf16[4,1024,128]{1,2,0:T(8,128)(2,1)S(1)} all-reduce(f32[4,1024,128]{1,2,0:T(8,128)S(1)} %fusion.47), channel_id=1, replica_groups=mesh['fac'=8,'freq'=4] {'fac'}, use_global_device_ids=true, to_apply=%region_2.0 | all-reduce | flops 524288 | bytes 3145728 | tf_op jit(solution)/shard_map/psum | solution.py:21
  736.8 19.6 %fusion.57 = f32[4,1024,128]{1,2,0:T(8,128)S(1)} fusion(bf16[4608,1024]{1,0:T(8,128)(2,1)} %param.7, f32[4,4608,128]{1,2,0:T(8,128)} %add.28, f32[4,4608]{1,0:T(4,128)S(1)} %copy-done.4, bf16[4,1024,128]{1,2,0:T(8,128)(2,1)S(1)} %all-reduce.6), kind=kOutput, calls=%fused_computation.40 | convolution fusion | flops 9670754304 | bytes 22093824 | tf_op jit(solution)/shard_map/pa,fpc->fac/dot_general | solution.py:18
  756.4 55.9 %all-reduce.7 = bf16[4,1024,128]{1,2,0:T(8,128)(2,1)S(1)} all-reduce(f32[4,1024,128]{1,2,0:T(8,128)S(1)} %fusion.57), channel_id=1, replica_groups=mesh['fac'=8,'freq'=4] {'fac'}, use_global_device_ids=true, to_apply=%region_3.0 | all-reduce | flops 524288 | bytes 3145728 | tf_op jit(solution)/shard_map/psum | solution.py:21
  812.3 12.6 bitcast_add_fusion.1
  825.0 11.8 copy.51
  836.8 208.6 %all_to_all.94 = f32[4,4608,128]{2,0,1:T(4,128)S(1)} all-to-all(f32[4,4608,128]{2,0,1:T(4,128)} %copy.51), channel_id=1, replica_groups=mesh['fac'=8,'freq'=4] {'freq'}, dimensions={1} | all-to-all | bytes 18874368 | tf_op jit(solution)/shard_map/all_to_all | solution.py:27
  1046.9 13.7 %fusion.20 = f32[1152,128,16]{1,2,0:T(8,128)S(1)} fusion(f32[16,1152,128]{2,1,0:T(8,128)S(1)} %bitcast.121, f32[16,16]{1,0:T(8,128)S(1)} %copy-done), kind=kOutput, calls=%fused_computation.27 | convolution fusion | flops 452984832 | bytes 18875392 | tf_op jit(solution)/shard_map/tw,wpc->tpc/dot_general | solution.py:30
  1060.6 10.5 fusion.37
  1071.1 6.5 copy.55
  1077.6 5.8 all-to-all-start.4
  1083.5 9.6 copy.57
  1093.0 196.4 %all-to-all-done.4 = f32[16,1152,128]{2,1,0:T(8,128)} async-done(((f32[16,1152,128]{2,1,0:T(8,128)}), f32[16,1152,128]{2,1,0:T(8,128)}, u32[]{:S(2)}, u32[]{:S(2)}) %all-to-all-start.4) | async-done | bytes 9437216 | tf_op jit(solution)/shard_map/all_to_all | solution.py:33
  1289.4 8.2 copy.56
  1297.7 11.0 bitcast_add_fusion
  (17 shorter events, 6.5 us)
Async XLA Ops:
  0.6 397.7 %copy-start = (f32[16,16]{1,0:T(8,128)S(1)}, f32[16,16]{1,0:T(8,128)}, u32[]{:S(2)}) copy-start(f32[16,16]{1,0:T(8,128)} %param.10) | copy-start | bytes 3076
  0.6 182.3 %all-to-all-start = ((f32[4,4,1152]{2,0,1:T(4,128)}), f32[4,4,1152]{2,0,1:T(4,128)S(1)}, u32[]{:S(2)}, u32[]{:S(2)}) async-start(f32[4,4,1152]{2,0,1:T(4,128)} %bitcast.123), calls=%async_computation | async-start | bytes 147456 | tf_op jit(solution)/shard_map/all_to_all | solution.py:28
  14.8 67.7 %copy-start.4 = (f32[4,4608]{1,0:T(4,128)S(1)}, f32[4,4608]{1,0:T(4,128)}, u32[]{:S(2)}) copy-start(f32[4,4608]{1,0:T(4,128)} %param.8) | copy-start | bytes 221188
  183.0 210.1 %all-to-all-start.1 = ((f32[4,4608,128]{2,0,1:T(4,128)}), f32[4,4608,128]{2,0,1:T(4,128)}, u32[]{:S(2)}, u32[]{:S(2)}) async-start(f32[4,4608,128]{2,0,1:T(4,128)} %copy.44), calls=%async_computation.1 | async-start | bytes 18874368 | tf_op jit(solution)/shard_map/all_to_all | solution.py:27
  398.3 13.9 %copy-start.1 = (f32[16,1152]{0,1:T(8,128)S(1)}, f32[16,1152]{0,1:T(8,128)}, u32[]{:S(2)}) copy-start(f32[16,1152]{0,1:T(8,128)} %copy.40) | copy-start | bytes 221188
  398.3 13.9 %copy-start.3 = (f32[16,16]{1,0:T(8,128)S(1)}, f32[16,16]{1,0:T(8,128)}, u32[]{:S(2)}) copy-start(f32[16,16]{1,0:T(8,128)} %param.11) | copy-start | bytes 3076
  1046.8 13.8 %copy-start.2 = (f32[16,1152]{0,1:T(8,128)S(1)}, f32[16,1152]{0,1:T(8,128)}, u32[]{:S(2)}) copy-start(f32[16,1152]{0,1:T(8,128)} %copy.40) | copy-start | bytes 221188
  1077.6 211.8 %all-to-all-start.4 = ((f32[16,1152,128]{2,1,0:T(8,128)}), f32[16,1152,128]{2,1,0:T(8,128)}, u32[]{:S(2)}, u32[]{:S(2)}) async-start(f32[16,1152,128]{2,1,0:T(8,128)} %copy.55), calls=%async_computation.4 | async-start | bytes 18874368 | tf_op jit(solution)/shard_map/all_to_all | solution.py:33
where the time goes:
time: 1320 us; the launch traced here: 1310 us
  blocking collectives  644 us (49%)
  waiting for transfers between devices  399 us (30%)
  matrix products  134 us (10%)
  local copies, waits for them, and re-layouts  91.6 us (7%)
  other arithmetic  22.8 us (2%)
  starting transfers between devices  16.4 us (1%)
    psum x4, blocking collectives, shards(): projected = lax.psum(partial_value, 'fac').astype(jnp.bfloat16)  225 us
    all_to_all x1, blocking collectives, shards(): lax.all_to_all(renewed, 'freq', split_axis=0, concat_axis=1, tiled=True)  210 us
    all_to_all x1, blocking collectives, shards(): lax.all_to_all(amplitude, 'freq', split_axis=1, concat_axis=0, tiled=True)  209 us
    all_to_all x1, waiting for transfers between devices, shards(): lax.all_to_all(amplitude, 'freq', split_axis=1, concat_axis=0, tiled=True)  203 us
    all_to_all x1, waiting for transfers between devices, shards(): lax.all_to_all(renewed, 'freq', split_axis=0, concat_axis=1, tiled=True)  196 us
    dot_general x4, matrix products, shards(): jnp.einsum('pa,fpc->fac', factors, rounded, preferred_element_type=jnp.fl...  59.9 us
    all_to_all x3, local copies, waits for them, and re-layouts, shards(): lax.all_to_all(renewed, 'freq', split_axis=0, concat_axis=1, tiled=True)  31.4 us
    dot_general x2, matrix products, shards(): jnp.einsum('tw,wpc->tpc', forward, moved, precision=lax.Precision.HIGHEST)  27.6 us
  transfers between devices with their start and end apart: 3, of which 2 were waited for; matrix products, arithmetic and copies ran while one was open for 6% of the time, Pallas kernels for 0%

commit v1 on v0

--- a/solution.py
+++ b/solution.py
@@ -18,7 +18,7 @@
             partial_value = jnp.einsum(
                 "pa,fpc->fac", factors, rounded, preferred_element_type=jnp.float32
             )
-            projected = lax.psum(partial_value, "fac").astype(jnp.bfloat16)
+            projected = jnp.sum(lax.all_gather(partial_value, "fac"), axis=0).astype(jnp.bfloat16)
             spread = jnp.einsum(
                 "pa,fac->fpc", factors, projected, preferred_element_type=jnp.float32
             )

time: 1320 us -> 1490 us (1.13)
  waiting for transfers between devices: 399 us -> 746 us
  blocking collectives: 644 us -> 418 us
  other arithmetic: 22.8 us -> 50.2 us
    all_gather x0 -> x4, waiting for transfers between devices: none -> 346 us  [shards(): lax.all_gather(partial_value, 'fac')]
    psum x4 -> x0, blocking collectives: 225 us -> none  [shards(): projected = lax.psum(partial_value, 'fac').astype(jnp.bfloat16)]
    reduce_sum x0 -> x4, other arithmetic: none -> 27.4 us  [shards(): jnp.sum(lax.all_gather(partial_value, 'fac'), axis=0).astype(jnp.bfloat16)]
  transfers between devices with their start and end apart: 3 -> 7, of which waited for: 2 -> 6; matrix products, arithmetic and copies ran while one was open for 6% -> 4% of each run, Pallas kernels for 0% -> 0%
where the time goes in v1:
time: 1490 us; the launch traced here: 1480 us
  waiting for transfers between devices  746 us (50%)
  blocking collectives  418 us (28%)
  matrix products  134 us (9%)
  local copies, waits for them, and re-layouts  99.9 us (7%)
  other arithmetic  50.2 us (3%)
  starting transfers between devices  16.8 us (1%)
    all_gather x4, waiting for transfers between devices, shards(): lax.all_gather(partial_value, 'fac')  346 us
    all_to_all x1, blocking collectives, shards(): lax.all_to_all(amplitude, 'freq', split_axis=1, concat_axis=0, tiled=True)  209 us
    all_to_all x1, blocking collectives, shards(): lax.all_to_all(renewed, 'freq', split_axis=0, concat_axis=1, tiled=True)  208 us
    all_to_all x1, waiting for transfers between devices, shards(): lax.all_to_all(amplitude, 'freq', split_axis=1, concat_axis=0, tiled=True)  204 us
    all_to_all x1, waiting for transfers between devices, shards(): lax.all_to_all(renewed, 'freq', split_axis=0, concat_axis=1, tiled=True)  196 us
    dot_general x4, matrix products, shards(): jnp.einsum('pa,fpc->fac', factors, rounded, preferred_element_type=jnp.fl...  59.7 us
    all_to_all x3, local copies, waits for them, and re-layouts, shards(): lax.all_to_all(renewed, 'freq', split_axis=0, concat_axis=1, tiled=True)  31.4 us
  transfers between devices with their start and end apart: 7, of which 6 were waited for; matrix products, arithmetic and copies ran while one was open for 4% of the time, Pallas kernels for 0%

profile of v1, /device:TPU:3, one launch (start us, length us, event | category | flops | bytes accessed | tf_op | source)
XLA Modules:
  0.0 1478.6 jit_solution(5861802933569559442)
XLA Ops:
  7.2 10.4 fusion.42
  19.5 9.6 copy.87
  29.2 81.8 %all-gather.9.cloned.1.call-done = f32[32,1024,128]{2,1,0:T(8,128)} async-done(((f32[4,1024,128]{2,1,0:T(8,128)}), f32[32,1024,128]{2,1,0:T(8,128)}) %all-gather.9.cloned.1.call-update) | async-done | bytes 16777232 | tf_op jit(solution)/shard_map/all_gather | solution.py:21
  111.0 6.9 reduce_sum.36
  118.4 19.5 %fusion.52 = f32[4,1024,128]{1,2,0:T(8,128)S(1)} fusion(bf16[4608,1024]{1,0:T(8,128)(2,1)} %param.7, f32[4,4608,128]{1,2,0:T(8,128)} %copy.87, f32[4,4608]{1,0:T(4,128)S(1)} %copy-done.4, bf16[4,1024,128]{1,2,0:T(8,128)(2,1)S(1)} %copy.102), kind=kOutput, calls=%fused_computation.39 | convolution fusion | flops 9670754304 | bytes 22093824 | tf_op jit(solution)/shard_map/pa,fpc->fac/dot_general | solution.py:18
  144.5 85.1 %all-gather.11.cloned.1.call-done = f32[32,1024,128]{2,1,0:T(8,128)} async-done(((f32[4,1024,128]{2,1,0:T(8,128)}), f32[32,1024,128]{2,1,0:T(8,128)}) %all-gather.11.cloned.1.call-update) | async-done | bytes 16777232 | tf_op jit(solution)/shard_map/all_gather | solution.py:21
  229.6 6.8 reduce_sum.37
  236.5 12.9 bitcast_add_fusion.3
  249.3 11.9 copy.81
  268.2 204.2 %all-to-all-done.1 = f32[4,4608,128]{2,0,1:T(4,128)} async-done(((f32[4,4608,128]{2,0,1:T(4,128)}), f32[4,4608,128]{2,0,1:T(4,128)}, u32[]{:S(2)}, u32[]{:S(2)}) %all-to-all-start.1) | async-done | bytes 9437216 | tf_op jit(solution)/shard_map/all_to_all | solution.py:27
  477.6 13.7 fusion.22
  491.3 10.5 fusion.36
  504.8 208.4 %all_to_all.93 = f32[16,1152,128]{2,1,0:T(8,128)} all-to-all(f32[16,1152,128]{2,1,0:T(8,128)S(1)} %copy.85), channel_id=1, replica_groups=mesh['fac'=8,'freq'=4] {'freq'}, dimensions={0} | all-to-all | bytes 18874368 | tf_op jit(solution)/shard_map/all_to_all | solution.py:33
  713.2 11.9 copy.86
  725.0 11.3 all_to_all.79
  736.3 11.8 add.20
  748.1 10.3 fusion.47
  760.6 89.4 %all-gather.13.cloned.1.call-done = f32[32,1024,128]{2,1,0:T(8,128)} async-done(((f32[4,1024,128]{2,1,0:T(8,128)}), f32[32,1024,128]{2,1,0:T(8,128)}) %all-gather.13.cloned.1.call-update) | async-done | bytes 16777232 | tf_op jit(solution)/shard_map/all_gather | solution.py:21
  850.0 6.8 reduce_sum.38
  857.4 19.5 %fusion.57 = f32[4,1024,128]{1,2,0:T(8,128)S(1)} fusion(bf16[4608,1024]{1,0:T(8,128)(2,1)} %param.7, f32[4,4608,128]{1,2,0:T(8,128)} %add.20, f32[4,4608]{1,0:T(4,128)S(1)} %copy-done.4, bf16[4,1024,128]{1,2,0:T(8,128)(2,1)S(1)} %copy.103), kind=kOutput, calls=%fused_computation.40 | convolution fusion | flops 9670754304 | bytes 22093824 | tf_op jit(solution)/shard_map/pa,fpc->fac/dot_general | solution.py:18
  878.7 89.9 %all-gather.15.cloned.1.call-done = f32[32,1024,128]{2,1,0:T(8,128)} async-done(((f32[4,1024,128]{2,1,0:T(8,128)}), f32[32,1024,128]{2,1,0:T(8,128)}) %all-gather.15.cloned.1.call-update) | async-done | bytes 16777232 | tf_op jit(solution)/shard_map/all_gather | solution.py:21
  968.6 6.8 reduce_sum.39
  975.4 12.9 bitcast_add_fusion.1
  988.3 11.8 copy.92
  1000.1 209.4 %all_to_all.94 = f32[4,4608,128]{2,0,1:T(4,128)S(1)} all-to-all(f32[4,4608,128]{2,0,1:T(4,128)} %copy.92), channel_id=1, replica_groups=mesh['fac'=8,'freq'=4] {'freq'}, dimensions={1} | all-to-all | bytes 18874368 | tf_op jit(solution)/shard_map/all_to_all | solution.py:27
  1211.0 13.7 fusion.20
  1224.7 10.5 fusion.37
  1235.1 6.5 copy.96
  1247.5 9.6 copy.98
  1257.1 195.5 %all-to-all-done.4 = f32[16,1152,128]{2,1,0:T(8,128)} async-done(((f32[16,1152,128]{2,1,0:T(8,128)}), f32[16,1152,128]{2,1,0:T(8,128)}, u32[]{:S(2)}, u32[]{:S(2)}) %all-to-all-start.4) | async-done | bytes 9437216 | tf_op jit(solution)/shard_map/all_to_all | solution.py:33
  1452.6 8.2 copy.97
  1460.8 11.0 bitcast_add_fusion
  (35 shorter events, 35.9 us)
Async XLA Ops:
  7.2 470.4 %copy-start = (f32[16,16]{1,0:T(8,128)S(1)}, f32[16,16]{1,0:T(8,128)}, u32[]{:S(2)}) copy-start(f32[16,16]{1,0:T(8,128)} %param.10) | copy-start | bytes 3076
  7.2 103.8 %all-gather.9.cloned.1.call-start = ((), (), s32[]{:S(2)}) async-start(), calls=%async_computation.5 | async-start | bytes 18874368 | tf_op jit(solution)/shard_map/all_gather | solution.py:21
  19.5 210.1 %all-gather.11.cloned.1.call-start = ((), (), s32[]{:S(2)}) async-start(), calls=%async_computation.6 | async-start | bytes 18874368 | tf_op jit(solution)/shard_map/all_gather | solution.py:21
  111.0 7.4 copy-start.4
  139.7 121.5 %all-to-all-start = ((f32[4,4,1152]{2,0,1:T(4,128)}), f32[4,4,1152]{2,0,1:T(4,128)S(1)}, u32[]{:S(2)}, u32[]{:S(2)}) async-start(f32[4,4,1152]{2,0,1:T(4,128)} %bitcast), calls=%async_computation | async-start | bytes 147456 | tf_op jit(solution)/shard_map/all_to_all | solution.py:28
  261.2 211.2 %all-to-all-start.1 = ((f32[4,4608,128]{2,0,1:T(4,128)}), f32[4,4608,128]{2,0,1:T(4,128)}, u32[]{:S(2)}, u32[]{:S(2)}) async-start(f32[4,4608,128]{2,0,1:T(4,128)} %copy.81), calls=%async_computation.1 | async-start | bytes 18874368 | tf_op jit(solution)/shard_map/all_to_all | solution.py:27
  267.0 583.0 %all-gather.13.cloned.1.call-start = ((), (), s32[]{:S(2)}) async-start(), calls=%async_computation.7 | async-start | bytes 18874368 | tf_op jit(solution)/shard_map/all_gather | solution.py:21
  477.6 13.7 copy-start.1
  477.6 13.7 copy-start.3
  760.3 208.2 %all-gather.15.cloned.1.call-start = ((), (), s32[]{:S(2)}) async-start(), calls=%async_computation.8 | async-start | bytes 18874368 | tf_op jit(solution)/shard_map/all_gather | solution.py:21
  1211.0 13.7 copy-start.2
  1241.7 210.9 %all-to-all-start.4 = ((f32[16,1152,128]{2,1,0:T(8,128)}), f32[16,1152,128]{2,1,0:T(8,128)}, u32[]{:S(2)}, u32[]{:S(2)}) async-start(f32[16,1152,128]{2,1,0:T(8,128)} %copy.96), calls=%async_computation.4 | async-start | bytes 18874368 | tf_op jit(solution)/shard_map/all_to_all | solution.py:33
Sparse Core Ops, SparseCore 0:
  19.6 91.3 all-gather.8
  139.9 89.7 all-gather.10
  760.4 89.5 all-gather.12
  878.8 89.7 all-gather.14
